TPU v7x, 32 devices: a whole 2x2x4 slice. The times are simulated.
32 devices in a mesh: req: 8 (over z, x), mlp: 4 (over y, core).
Axes of the slice: x: 2, y: 2, z: 4, core: 2. Of those that a mesh axis runs over, the one named last changes fastest.
Arguments:
- tokens: bfloat16 [8192, 2048], P('req', 'mlp'), may hold values from -40 to 40, as said below
- norm_gain_vector: bfloat16 [2048], replicated, may hold values from 0.099609375 to 1.8984375
- gate_weight: bfloat16 [2048, 3584], P(None, 'mlp'), may hold values from -0.125 to 0.125
- up_weight: bfloat16 [2048, 3584], P(None, 'mlp'), may hold values from -0.125 to 0.125
- down_weight: bfloat16 [3584, 2048], P('mlp'), may hold values from -0.09375 to 0.09375
- gate_up_input_maps: bfloat16 [8, 2048, 32], P('req'), may hold values from -0.125 to 0.125
- gate_up_output_maps: bfloat16 [8, 2, 16, 3584], P('req', None, None, 'mlp'), may hold values from -1.5 to 1.5
- down_input_maps: bfloat16 [8, 3584, 16], P('req', 'mlp'), may hold values from -0.09375 to 0.09375
- down_output_maps: bfloat16 [8, 16, 2048], P('req'), may hold values from -1.5 to 1.5
- lengths: int32 [8, 4], replicated, may hold values from 0 to 1024, as said below
- request_adapter_slot: int32 [8, 4], replicated, may hold values from 0 to 7
- selected: int32 [8], replicated, may hold values from 0 to 7, as said below
Outputs:
- layer_out: bfloat16 [8192, 2048], P('req', 'mlp')
Inputs may be any that keep to these rules, and one draw needn't show every extreme that they name: Each row of lengths sums to a multiple of 64 from 64 to 1024; some row sums to exactly 1024 and holds all of it in one slot; all rows together sum to 4096. Slots may hold zero tokens. `selected`: 8 different adapter ids; adapter a is owned by index a // 1 of req. `tokens`: entries of order one, some rows and features larger than others.
All inputs are finite; a program needn't handle non-finite values.
Results may differ from a plain program's by a relative error of at most 0.006.
Values may be sent and summed in bfloat16 or wider, within the bound.
A program may use at most 128 MiB of HBM per device.

v0:
```python
import jax
import jax.numpy as jnp
from jax import lax
from jax.sharding import PartitionSpec as P

TOK_DEV = 512
EPSILON = 1e-06


def gather_adapter_maps(gate_up_input_maps, gate_up_output_maps, down_input_maps, down_output_maps):
    token_count = gate_up_input_maps.shape[0]
    return jnp.concatenate(
        [
            gate_up_input_maps.reshape(token_count, -1),
            gate_up_output_maps.reshape(token_count, -1),
            down_input_maps.reshape(token_count, -1),
            down_output_maps.reshape(token_count, -1),
        ],
        axis=1,
    )


def unpack_adapters(packed_adapters, width_size, rank_size, inner_hidden):
    token_count = packed_adapters.shape[0]
    first_branch = width_size * 2 * rank_size
    second_branch = first_branch + 2 * rank_size * inner_hidden
    third = second_branch + inner_hidden * rank_size
    gate_up_input_maps = packed_adapters[:, :first_branch].reshape(
        token_count, width_size, 2 * rank_size
    )
    gate_up_output_maps = packed_adapters[:, first_branch:second_branch].reshape(
        token_count, 2, rank_size, inner_hidden
    )
    down_input_maps = packed_adapters[:, second_branch:third].reshape(
        token_count, inner_hidden, rank_size
    )
    down_output_maps = packed_adapters[:, third:].reshape(token_count, rank_size, width_size)
    return (gate_up_input_maps, gate_up_output_maps, down_input_maps, down_output_maps)


def slot_table(owners, positions, lengths, request_adapter_slot, token_count):
    lens = jnp.take(lengths, owners, axis=0)
    req_ends = jnp.cumsum(lens, axis=1)
    starts = req_ends - lens
    inside = (positions[:, None] >= starts) & (positions[:, None] < req_ends)
    adapter_ids = jnp.take(request_adapter_slot, owners, axis=0)
    picked = jnp.sum(jnp.where(inside, adapter_ids, 0), axis=1)
    live = jnp.any(inside, axis=1)
    onehot = (picked[:, None] == jnp.arange(token_count, dtype=jnp.int32)[None, :]) & live[:, None]
    return onehot.astype(jnp.float32)


def mlp_partial(
    whole, norm_gain_vector, gate_weight, up_weight, down_weight, adapter_table, onehot
):
    gate_up_input_maps, gate_up_output_maps, down_input_maps, down_output_maps = adapter_table
    rank_size = down_output_maps.shape[1]
    values = whole.astype(jnp.float32)
    mean_square = jnp.mean(values * values, axis=1, keepdims=True)
    normed_input = (
        values * lax.rsqrt(mean_square + EPSILON) * norm_gain_vector.astype(jnp.float32)
    ).astype(jnp.bfloat16)
    low_rank_term = jnp.einsum(
        "ec,mch->emh", normed_input, gate_up_input_maps, preferred_element_type=jnp.float32
    )
    low_rank_term = (low_rank_term * onehot[:, :, None]).astype(jnp.bfloat16)
    gate_sum = jnp.dot(normed_input, gate_weight, preferred_element_type=jnp.float32) + jnp.einsum(
        "vca,can->vn",
        low_rank_term[:, :, :rank_size],
        gate_up_output_maps[:, 0],
        preferred_element_type=jnp.float32,
    )
    up_sum = jnp.dot(normed_input, up_weight, preferred_element_type=jnp.float32) + jnp.einsum(
        "vca,can->vn",
        low_rank_term[:, :, rank_size:],
        gate_up_output_maps[:, 1],
        preferred_element_type=jnp.float32,
    )
    hidden = (jax.nn.silu(gate_sum) * up_sum).astype(jnp.bfloat16)
    down_rank = (
        jnp.einsum("tf,sfr->tsr", hidden, down_input_maps, preferred_element_type=jnp.float32)
        * onehot[:, :, None]
    )
    down_term = jnp.einsum(
        "tsr,srd->td",
        down_rank,
        down_output_maps.astype(jnp.float32),
        precision=lax.Precision.HIGHEST,
        preferred_element_type=jnp.float32,
    )
    return jnp.dot(hidden, down_weight, preferred_element_type=jnp.float32) + down_term


def on_device(
    tokens,
    norm_gain_vector,
    gate_weight,
    up_weight,
    down_weight,
    gate_up_input_maps,
    gate_up_output_maps,
    down_input_maps,
    down_output_maps,
    lengths,
    request_adapter_slot,
    selected,
):
    groups = lax.axis_size("req")
    device = lax.axis_index("req")
    capacity, columns = tokens.shape
    chosen_count = selected.shape[0]
    rank_size = down_output_maps.shape[1]
    width_size = down_output_maps.shape[2]
    inner_hidden = down_input_maps.shape[1]
    packed_adapters = gather_adapter_maps(
        gate_up_input_maps, gate_up_output_maps, down_input_maps, down_output_maps
    )
    every = lax.all_gather(packed_adapters, "req", axis=0, tiled=True)
    chosen = jnp.take(every, selected, axis=0)
    adapter_table = unpack_adapters(chosen, width_size, rank_size, inner_hidden)
    totals = jnp.sum(lengths, axis=1)
    block_rows = TOK_DEV // groups
    spread = capacity // TOK_DEV
    counts = totals // block_rows
    group_ends = jnp.cumsum(counts)
    offsets = group_ends - counts
    turn_by = offsets[device] % groups
    blocks = tokens.reshape(spread, groups, block_rows, columns)
    outgoing = jnp.roll(blocks, turn_by, axis=1)
    incoming = lax.all_to_all(outgoing, "req", split_axis=1, concat_axis=1, tiled=True)
    places = jnp.arange(groups, dtype=jnp.int32)
    global_ids = places * groups + device
    owners = jnp.sum((group_ends[None, :] <= global_ids[:, None]).astype(jnp.int32), axis=1)
    inner_ids = global_ids - jnp.take(offsets, owners)
    indices = inner_ids // groups * groups + owners
    flat_blocks = incoming.reshape(spread * groups, block_rows, columns)
    balanced = jnp.take(flat_blocks, indices, axis=0).reshape(groups * block_rows, columns)
    row_owner = jnp.repeat(owners, block_rows)
    row_position = (
        inner_ids[:, None] * block_rows + jnp.arange(block_rows, dtype=jnp.int32)[None, :]
    ).reshape(-1)
    onehot = slot_table(row_owner, row_position, lengths, request_adapter_slot, chosen_count)
    whole = lax.all_gather(balanced, "mlp", axis=1, tiled=True)
    partial_value = mlp_partial(
        whole, norm_gain_vector, gate_weight, up_weight, down_weight, adapter_table, onehot
    )
    branch = lax.psum_scatter(
        partial_value.astype(jnp.bfloat16), "mlp", scatter_dimension=1, tiled=True
    )
    back = (
        jnp.zeros((spread * groups, block_rows, columns), jnp.bfloat16)
        .at[indices]
        .set(branch.reshape(groups, block_rows, columns))
    )
    returned = lax.all_to_all(
        back.reshape(spread, groups, block_rows, columns),
        "req",
        split_axis=1,
        concat_axis=1,
        tiled=True,
    )
    branch_rows = jnp.roll(returned, -turn_by, axis=1).reshape(capacity, columns)
    branch_rows = lax.optimization_barrier(branch_rows).astype(jnp.float32)
    row_valid = jnp.arange(capacity, dtype=jnp.int32) < totals[device]
    values = tokens.astype(jnp.float32)
    return jnp.where(row_valid[:, None], values + branch_rows, values).astype(jnp.bfloat16)


def solution(mesh):
    in_specs = (
        P("req", "mlp"),
        P(),
        P(None, "mlp"),
        P(None, "mlp"),
        P("mlp", None),
        P("req", None, None),
        P("req", None, None, "mlp"),
        P("req", "mlp", None),
        P("req", None, None),
        P(),
        P(),
        P(),
    )
    out_specs = P("req", "mlp")
    return jax.shard_map(
        on_device, mesh=mesh, in_specs=in_specs, out_specs=out_specs, check_vma=False
    )
```

profile of v0, /device:TPU:0, one launch (start us, length us, event | category | flops | bytes accessed | tf_op | source)
XLA Modules:
  0.0 234.6 jit_solution(14905129458668095679)
XLA Ops:
  6.5 1.3 copy.45
  7.8 0.3 reshape.318
  8.1 0.9 copy.46
  9.2 0.9 copy.62
  10.3 7.0 %maximum_bitcast_fusion = bf16[1,1,141312]{2,1,0:T(2,128)(2,1)} fusion(bf16[1,32768]{1,0:T(2,128)(2,1)S(1)} %bitcast.101, bf16[1,14336]{1,0:T(2,128)(2,1)S(1)} %reshape.320, bf16[1,28672]{1,0:T(2,128)(2,1)S(1)} %bitcast.104, bf16[1,65536]{1,0:T(2,128)(2,1)S(1)} %reshape.318), kind=kLoop, calls=%fused_computation.28 | loop fusion | flops 1130496 | bytes 565248
  17.6 0.6 dynamic_slice.10
  20.1 0.4 fusion.8
  20.6 1.0 copy.43
  21.6 7.3 %all-to-all-start = ((bf16[2,8,64,512]{3,2,0,1:T(8,128)(2,1)}), bf16[2,8,64,512]{3,2,0,1:T(8,128)(2,1)S(1)}, u32[]{:S(2)}, u32[]{:S(2)}) async-start(bf16[2,8,64,512]{3,2,0,1:T(8,128)(2,1)} %copy.43), calls=%async_computation | async-start | bytes 2097152 | tf_op jit(solution)/shard_map/all_to_all | solution.py:130
  29.2 0.6 gather_fusion
  30.4 1.0 gather_fusion.4
  31.9 1.0 gather_fusion.5
  33.0 0.3 fusion.31
  33.3 0.2 fusion.11
  33.5 39.2 %all-to-all-done = bf16[2,8,64,512]{3,2,0,1:T(8,128)(2,1)S(1)} async-done(((bf16[2,8,64,512]{3,2,0,1:T(8,128)(2,1)}), bf16[2,8,64,512]{3,2,0,1:T(8,128)(2,1)S(1)}, u32[]{:S(2)}, u32[]{:S(2)}) %all-to-all-start) | async-done | bytes 1048608 | tf_op jit(solution)/shard_map/all_to_all | solution.py:130
  72.8 0.6 gather_fusion.1
  73.4 1.0 bitcast_select_fusion
  74.4 0.2 reduce-scatter.2.cloned.1.call-start
  74.7 43.2 %all-gather.6.cloned.1.call-done = bf16[8,1,141312]{2,1,0:T(2,128)(2,1)} async-done(((bf16[1,1,141312]{2,1,0:T(2,128)(2,1)}), bf16[8,1,141312]{2,1,0:T(2,128)(2,1)}) %all-gather.6.cloned.1.call-update) | async-done | bytes 2261008 | tf_op jit(solution)/shard_map/all_gather | solution.py:118
  117.9 3.4 %copy.70 = bf16[8,1,141312]{2,0,1:T(8,128)(2,1)S(1)} copy(bf16[8,1,141312]{2,1,0:T(2,128)(2,1)} %all-gather.6.cloned.1.call-done) | data formatting | bytes 4521984
  121.5 1.3 gather_fusion.2
  122.8 2.3 gather_fusion.3
  125.1 4.4 %maximum_select_fusion = bf16[8,141312]{1,0:T(8,128)(2,1)S(1)} fusion(bf16[8,70656]{1,0:T(8,128)(2,1)} %gather_fusion.3, bf16[8,70656]{1,0:T(8,128)(2,1)S(1)} %gather_fusion.2, pred[8]{0:T(512)(128)(4,1)S(1)} %get-tuple-element.13), kind=kLoop, calls=%fused_computation.15 | loop fusion | flops 5652480 | bytes 4521992 | tf_op jit(solution)/shard_map/jit(_take)/select_n | solution.py:119
  129.6 1.3 copy-done
  130.9 5.0 %reshape.322 = bf16[8,2048,32]{2,1,0:T(8,128)(2,1)} reshape(bf16[8,65536]{1,0:T(8,128)(2,1)S(1)} %slice.44) | data formatting | bytes 2097152 | tf_op jit(solution)/shard_map/reshape | solution.py:28
  136.0 4.6 %copy.47 = bf16[8,2048,32]{1,2,0:T(8,128)(2,1)} copy(bf16[8,2048,32]{2,1,0:T(8,128)(2,1)} %reshape.322) | data formatting | bytes 2097152 | tf_op jit(solution)/shard_map/reshape | solution.py:28
  140.7 1.5 reshape.325
  142.1 0.9 copy.52
  143.1 2.2 fusion
  145.4 2.1 fusion.27
  147.5 0.4 fusion.14
  147.9 1.6 copy-done.9
  149.5 2.4 %fusion.29 = f32[512,896]{1,0:T(8,128)S(1)} fusion(bf16[2048,896]{1,0:T(8,128)(2,1)S(1)} %copy-done.9, bf16[512,2048]{1,0:T(8,128)(2,1)S(1)} %copy-done.3, f32[2048]{0:T(1024)S(1)} %convert_element_type.41, f32[512]{0:T(512)S(1)} %add_rsqrt_fusion), kind=kOutput, calls=%fused_computation.94 | convolution fusion | flops 1883242496 | bytes 7612416 | tf_op jit(solution)/shard_map/dot_general | solution.py:67
  151.9 2.4 %fusion.25 = f32[512,896]{1,0:T(8,128)S(1)} fusion(bf16[2048,896]{1,0:T(8,128)(2,1)S(1)} %copy-done.10, bf16[512,2048]{1,0:T(8,128)(2,1)S(1)} %copy-done.3, f32[2048]{0:T(1024)S(1)} %convert_element_type.41, f32[512]{0:T(512)S(1)} %add_rsqrt_fusion), kind=kOutput, calls=%fused_computation.92 | convolution fusion | flops 1883242496 | bytes 7612416 | tf_op jit(solution)/shard_map/dot_general | solution.py:73
  154.3 0.8 fusion.6
  155.1 0.4 fusion.36
  155.6 0.8 copy-done.11
  156.4 2.3 fusion.35
  158.7 3.5 %fusion.3 = bf16[512,2048]{1,0:T(8,128)(2,1)} fusion(f32[512,2048]{1,0:T(8,128)S(1)} %fusion.35, bf16[1,8,16,2048]{3,1,2,0:T(8,128)(2,1)S(1)} %bitcast.93, f32[512,8,16]{0,2,1:T(8,128)S(1)} %bitcast.107, f32[512,8]{0,1:T(8,128)S(1)} %fusion.19), kind=kOutput, calls=%fused_computation.13 | convolution fusion | flops 1612775424 | bytes 7094272 | tf_op jit(solution)/shard_map/tsr,srd->td/dot_general | solution.py:84
  162.2 29.7 %reduce-scatter.2.cloned.1.call-done = bf16[512,512]{1,0:T(8,128)(2,1)} async-done(((bf16[512,2048]{1,0:T(8,128)(2,1)}), bf16[512,512]{1,0:T(8,128)(2,1)}) %reduce-scatter.2.cloned.1.call-update) | async-done | bytes 524304 | tf_op jit(solution)/shard_map/reduce_scatter | solution.py:147
  192.0 1.8 scatter_fusion
  193.8 1.1 copy.53
  194.9 5.5 %all-to-all-start.1 = ((bf16[2,8,64,512]{3,2,0,1:T(8,128)(2,1)}), bf16[2,8,64,512]{3,2,0,1:T(8,128)(2,1)S(1)}, u32[]{:S(2)}, u32[]{:S(2)}) async-start(bf16[2,8,64,512]{3,2,0,1:T(8,128)(2,1)} %copy.53), calls=%async_computation.2 | async-start | bytes 2097152 | tf_op jit(solution)/shard_map/all_to_all | solution.py:155
  200.4 0.6 dynamic_slice.9
  201.0 0.6 iota_compare_fusion.1
  201.7 24.5 %all-to-all-done.1 = bf16[2,8,64,512]{3,2,0,1:T(8,128)(2,1)S(1)} async-done(((bf16[2,8,64,512]{3,2,0,1:T(8,128)(2,1)}), bf16[2,8,64,512]{3,2,0,1:T(8,128)(2,1)S(1)}, u32[]{:S(2)}, u32[]{:S(2)}) %all-to-all-start.1) | async-done | bytes 1048608 | tf_op jit(solution)/shard_map/all_to_all | solution.py:155
  226.2 0.4 fusion.7
  226.7 1.4 fusion.4
  (72 shorter events, 2.5 us)
Async XLA Ops:
  6.5 3.7 %copy-start.4 = (bf16[1,2,16,896]{3,2,1,0:T(8,128)(2,1)S(1)}, bf16[1,2,16,896]{3,2,1,0:T(8,128)(2,1)}, u32[]{:S(2)}) copy-start(bf16[1,2,16,896]{3,2,1,0:T(8,128)(2,1)} %param.22) | copy-start | bytes 172036
  6.5 10.8 %copy-start.5 = (s32[8,4]{0,1:T(4,128)S(1)}, s32[8,4]{0,1:T(4,128)}, u32[]{:S(2)}) copy-start(s32[8,4]{0,1:T(4,128)} %param.25) | copy-start | bytes 388
  6.5 13.6 %copy-start.1 = (bf16[1024,512]{1,0:T(8,128)(2,1)S(1)}, bf16[1024,512]{1,0:T(8,128)(2,1)}, u32[]{:S(2)}) copy-start(bf16[1024,512]{1,0:T(8,128)(2,1)} %param.16) | copy-start | bytes 3145732
  6.5 111.3 %all-gather.6.cloned.1.call-start = ((), (), s32[]{:S(2)}) async-start(), calls=%async_computation.5 | async-start | bytes 5087232 | tf_op jit(solution)/shard_map/all_gather | solution.py:118
  20.5 9.3 %copy-start.8 = (s32[8]{0:T(128)S(1)}, s32[8]{0:T(128)}, u32[]{:S(2)}) copy-start(s32[8]{0:T(128)} %param.27) | copy-start | bytes 100
  20.5 9.5 %copy-start.6 = (bf16[2048]{0:T(1024)(128)(2,1)S(1)}, bf16[2048]{0:T(1024)(128)(2,1)}, u32[]{:S(2)}) copy-start(bf16[2048]{0:T(1024)(128)(2,1)} %param.17) | copy-start | bytes 12292
  21.6 51.1 %all-to-all-start = ((bf16[2,8,64,512]{3,2,0,1:T(8,128)(2,1)}), bf16[2,8,64,512]{3,2,0,1:T(8,128)(2,1)S(1)}, u32[]{:S(2)}, u32[]{:S(2)}) async-start(bf16[2,8,64,512]{3,2,0,1:T(8,128)(2,1)} %copy.43), calls=%async_computation | async-start | bytes 2097152 | tf_op jit(solution)/shard_map/all_to_all | solution.py:130
  28.8 2.9 %copy-start.7 = (s32[8,4]{0,1:T(4,128)S(1)}, s32[8,4]{0,1:T(4,128)}, u32[]{:S(2)}) copy-start(s32[8,4]{0,1:T(4,128)} %param.26) | copy-start | bytes 388
  28.8 114.3 %all-gather.4.cloned.1.call-start = ((), (), s32[]{:S(2)}) async-start(), calls=%async_computation.3 | async-start | bytes 2621440 | tf_op jit(solution)/shard_map/all_gather | solution.py:143
  74.4 117.5 %reduce-scatter.2.cloned.1.call-start = ((), (), s32[]{:S(2)}) async-start(), calls=%async_computation.4 | async-start | bytes 2621440 | tf_op jit(solution)/shard_map/reduce_scatter | solution.py:147
  129.5 1.4 copy-start
  136.0 4.6 %slice-start = ((bf16[8,141312]{1,0:T(8,128)(2,1)}), bf16[8,28672]{1,0:T(8,128)(2,1)S(1)}, s32[]{:S(2)}) async-start(bf16[8,141312]{1,0:T(8,128)(2,1)} %copy-done), calls=%async_computation.6 | async-start | bytes 917504 | tf_op jit(solution)/shard_map/slice | solution.py:31
  136.0 4.7 %slice-start.1 = ((bf16[8,141312]{1,0:T(8,128)(2,1)}), bf16[8,14336]{1,0:T(8,128)(2,1)S(1)}, s32[]{:S(2)}) async-start(bf16[8,141312]{1,0:T(8,128)(2,1)} %copy-done), calls=%async_computation.7 | async-start | bytes 458752 | tf_op jit(solution)/shard_map/slice | solution.py:34
  143.1 2.2 copy-start.3
  147.5 2.0 copy-start.9
  149.5 2.4 %copy-start.10 = (bf16[2048,896]{1,0:T(8,128)(2,1)S(1)}, bf16[2048,896]{1,0:T(8,128)(2,1)}, u32[]{:S(2)}) copy-start(bf16[2048,896]{1,0:T(8,128)(2,1)} %param.19) | copy-start | bytes 11010052
  154.3 2.0 copy-start.11
  156.4 2.3 slice-start.2
  194.9 31.3 %all-to-all-start.1 = ((bf16[2,8,64,512]{3,2,0,1:T(8,128)(2,1)}), bf16[2,8,64,512]{3,2,0,1:T(8,128)(2,1)S(1)}, u32[]{:S(2)}, u32[]{:S(2)}) async-start(bf16[2,8,64,512]{3,2,0,1:T(8,128)(2,1)} %copy.53), calls=%async_computation.2 | async-start | bytes 2097152 | tf_op jit(solution)/shard_map/all_to_all | solution.py:155
  201.7 25.0 %copy-start.2 = (bf16[1024,512]{1,0:T(8,128)(2,1)S(1)}, bf16[1024,512]{1,0:T(8,128)(2,1)}, u32[]{:S(2)}) copy-start(bf16[1024,512]{1,0:T(8,128)(2,1)} %param.16) | copy-start | bytes 3145732
Sparse Core Ops, SparseCore 0:
  17.4 100.3 all-gather.5
  119.4 20.7 all-gather.3
  162.3 29.5 reduce-scatter.1
where the time goes:
time: 235 us
  waiting for transfers between devices  137 us (58%)
  local copies, waits for them, and re-layouts  36.1 us (15%)
  other arithmetic  19 us (8%)
  between operations  15.5 us (7%)
  matrix products  14.2 us (6%)
  starting transfers between devices  13 us (6%)
    all_gather x1, waiting for transfers between devices, on_device(): every = lax.all_gather(packed_adapters, 'req', axis=0, tiled=True)  43.2 us
    all_to_all x1, waiting for transfers between devices, on_device(): lax.all_to_all(outgoing, 'req', split_axis=1, concat_axis=1, tiled=True)  39.2 us
    reduce_scatter x1, waiting for transfers between devices, on_device(): lax.psum_scatter(partial_value.astype(jnp.bfloat16), 'mlp', scatter_dimen...  29.7 us
    all_to_all x1, waiting for transfers between devices, on_device(): lax.all_to_all(back.reshape(spread, groups, block_rows, columns), 'req',...  24.5 us
    unnamed x33, local copies, waits for them, and re-layouts  10.7 us
    reshape x2, local copies, waits for them, and re-layouts, unpack_adapters(): packed_adapters[:, :first_branch]  9.65 us
    all_to_all x1, starting transfers between devices, on_device(): lax.all_to_all(outgoing, 'req', split_axis=1, concat_axis=1, tiled=True)  7.25 us
    unnamed x1, other arithmetic  6.99 us
  transfers between devices with their start and end apart: 5, of which 4 were waited for; matrix products, arithmetic and copies ran while one was open for 14% of the time, Pallas kernels for 0%

commit v1 on v0

--- a/solution.py
+++ b/solution.py
@@ -2,6 +2,7 @@
 import jax.numpy as jnp
 from jax import lax
 from jax.sharding import PartitionSpec as P
+from jax.lax import axis_index, axis_size, ppermute
 
 TOK_DEV = 512
 EPSILON = 1e-06
@@ -115,7 +116,29 @@
     packed_adapters = gather_adapter_maps(
         gate_up_input_maps, gate_up_output_maps, down_input_maps, down_output_maps
     )
-    every = lax.all_gather(packed_adapters, "req", axis=0, tiled=True)
+    y2 = axis_index("req")
+    now = axis_size("req")
+    small, near, all_values = (now, y2, packed_adapters.shape[0])
+    every = lax.dynamic_update_slice_in_dim(
+        jnp.zeros(
+            [q * small if h == 0 else q for h, q in enumerate(packed_adapters.shape)],
+            packed_adapters.dtype,
+        ),
+        packed_adapters,
+        near * all_values,
+        axis=0,
+    )
+    taken_in = mat_out = packed_adapters
+    for j in [*range(1, small // 2 + 1)]:
+        taken_in = ppermute(taken_in, "req", [(h, (h + 1) % small) for h in range(small)])
+        every = lax.dynamic_update_slice_in_dim(
+            every, taken_in, (near - j) % small * all_values, axis=0
+        )
+        if 2 * j < small:
+            mat_out = ppermute(mat_out, "req", [(h, (h - 1) % small) for h in range(small)])
+            every = lax.dynamic_update_slice_in_dim(
+                every, mat_out, (near + j) % small * all_values, axis=0
+            )
     chosen = jnp.take(every, selected, axis=0)
     adapter_table = unpack_adapters(chosen, width_size, rank_size, inner_hidden)
     totals = jnp.sum(lengths, axis=1)

time: 235 us -> 300 us (1.28)
  local copies, waits for them, and re-layouts: 36.1 us -> 127 us
  waiting for transfers between devices: 137 us -> 103 us
  starting transfers between devices: 13 us -> 24.2 us
  other arithmetic: 19 us -> 12.1 us
    dynamic_update_slice x0 -> x8, local copies, waits for them, and re-layouts: none -> 90.4 us  [the longest x4 45.2 us: on_device(): lax.dynamic_update_slice_in_dim(every, taken_in, (near - j) % small * all...]
    all_gather x1 -> x0, waiting for transfers between devices: 43.2 us -> none  [on_device(): every = lax.all_gather(packed_adapters, 'req', axis=0, tiled=True)]
    ppermute x0 -> x7, waiting for transfers between devices: none -> 41.3 us  [the longest x4 29.4 us: on_device(): ppermute(taken_in, 'req', [(h, (h + 1) % small) for h in range(small)])]
    all_to_all x1, waiting for transfers between devices: 39.2 us -> 0.01 us  [on_device(): lax.all_to_all(outgoing, 'req', split_axis=1, concat_axis=1, tiled=True)]
    ppermute x0 -> x7, starting transfers between devices: none -> 14.2 us  [the longest x4 7.96 us: on_device(): ppermute(taken_in, 'req', [(h, (h + 1) % small) for h in range(small)])]
    unnamed x1 -> x0, other arithmetic: 6.99 us -> none
    all_gather x1, waiting for transfers between devices: 0.02 us -> 5.88 us  [on_device(): whole = lax.all_gather(balanced, 'mlp', axis=1, tiled=True)]
    unnamed x33 -> x37, local copies, waits for them, and re-layouts: 10.7 us -> 7.03 us
  transfers between devices with their start and end apart: 5 -> 11, of which waited for: 4 -> 6; matrix products, arithmetic and copies ran while one was open for 14% -> 41% of each run, Pallas kernels for 0% -> 0%
where the time goes in v1:
time: 300 us; the launch traced here: 297 us
  local copies, waits for them, and re-layouts  127 us (42%)
  waiting for transfers between devices  103 us (34%)
  starting transfers between devices  24.2 us (8%)
  between operations  16 us (5%)
  matrix products  14.2 us (5%)
  other arithmetic  12.1 us (4%)
    dynamic_update_slice x4, local copies, waits for them, and re-layouts, on_device(): lax.dynamic_update_slice_in_dim(every, taken_in, (near - j) % small * all...  45.2 us
    dynamic_update_slice x3, local copies, waits for them, and re-layouts, on_device(): lax.dynamic_update_slice_in_dim(every, mat_out, (near + j) % small * all_...  33.9 us
    reduce_scatter x1, waiting for transfers between devices, on_device(): lax.psum_scatter(partial_value.astype(jnp.bfloat16), 'mlp', scatter_dimen...  31.6 us
    ppermute x4, waiting for transfers between devices, on_device(): ppermute(taken_in, 'req', [(h, (h + 1) % small) for h in range(small)])  29.4 us
    all_to_all x1, waiting for transfers between devices, on_device(): lax.all_to_all(back.reshape(spread, groups, block_rows, columns), 'req',...  24.5 us
    ppermute x3, waiting for transfers between devices, on_device(): ppermute(mat_out, 'req', [(h, (h - 1) % small) for h in range(small)])  11.9 us
    dynamic_update_slice x1, local copies, waits for them, and re-layouts, on_device(): lax.dynamic_update_slice_in_dim(jnp.zeros([q * small if h == 0 else q for...  11.3 us
    reshape x2, local copies, waits for them, and re-layouts, unpack_adapters(): packed_adapters[:, :first_branch]  9.66 us
  transfers between devices with their start and end apart: 11, of which 6 were waited for; matrix products, arithmetic and copies ran while one was open for 41% of the time, Pallas kernels for 0%

profile of v1, /device:TPU:0, one launch (start us, length us, event | category | flops | bytes accessed | tf_op | source)
XLA Modules:
  0.0 297.0 jit_solution(14311954195241612336)
XLA Ops:
  6.5 1.3 copy.47
  8.4 0.9 copy.62
  10.2 3.0 %collective-permute-start = (bf16[1,141312]{1,0:T(2,128)(2,1)S(1)}, bf16[1,141312]{1,0:T(2,128)(2,1)S(1)}, u32[]{:S(2)}, u32[]{:S(2)}) collective-permute-start(bf16[1,141312]{1,0:T(2,128)(2,1)S(1)} %constant_dynamic-update-slice_fusion), channel_id=1, source_target_pairs={{0,4},{4,8},{8,12},{12,16},{16,20},{20,24},{24,28},{28,0},{1,5},{5... | collective-permute-start | bytes 847880 | tf_op jit(solution)/shard_map/ppermute | solution.py:133
  13.2 3.1 %collective-permute-start.1 = (bf16[1,141312]{1,0:T(2,128)(2,1)S(1)}, bf16[1,141312]{1,0:T(2,128)(2,1)S(1)}, u32[]{:S(2)}, u32[]{:S(2)}) collective-permute-start(bf16[1,141312]{1,0:T(2,128)(2,1)S(1)} %constant_dynamic-update-slice_fusion), channel_id=1, source_target_pairs={{0,28},{4,0},{8,4},{12,8},{16,12},{20,16},{24,20},{28,24},{1,29},{... | collective-permute-start | bytes 847880 | tf_op jit(solution)/shard_map/ppermute | solution.py:138
  19.5 1.0 copy.45
  20.5 4.3 %all-to-all-start = ((bf16[2,8,64,512]{3,2,0,1:T(8,128)(2,1)}), bf16[2,8,64,512]{3,2,0,1:T(8,128)(2,1)}, u32[]{:S(2)}, u32[]{:S(2)}) async-start(bf16[2,8,64,512]{3,2,0,1:T(8,128)(2,1)} %copy.45), calls=%async_computation | async-start | bytes 2097152 | tf_op jit(solution)/shard_map/all_to_all | solution.py:153
  26.1 1.0 gather_fusion.4
  27.3 18.1 %collective-permute-done = bf16[1,141312]{1,0:T(2,128)(2,1)S(1)} collective-permute-done((bf16[1,141312]{1,0:T(2,128)(2,1)S(1)}, bf16[1,141312]{1,0:T(2,128)(2,1)S(1)}, u32[]{:S(2)}, u32[]{:S(2)}) %collective-permute-start) | collective-permute-done | bytes 282656 | tf_op jit(solution)/shard_map/ppermute | solution.py:133
  45.4 2.5 collective-permute-start.2
  48.3 1.0 gather_fusion.5
  49.6 11.9 %collective-permute-done.1 = bf16[1,141312]{1,0:T(2,128)(2,1)S(1)} collective-permute-done((bf16[1,141312]{1,0:T(2,128)(2,1)S(1)}, bf16[1,141312]{1,0:T(2,128)(2,1)S(1)}, u32[]{:S(2)}, u32[]{:S(2)}) %collective-permute-start.1) | collective-permute-done | bytes 282656 | tf_op jit(solution)/shard_map/ppermute | solution.py:138
  61.6 11.3 %collective-permute-done.2 = bf16[1,141312]{1,0:T(2,128)(2,1)S(1)} collective-permute-done((bf16[1,141312]{1,0:T(2,128)(2,1)S(1)}, bf16[1,141312]{1,0:T(2,128)(2,1)S(1)}, u32[]{:S(2)}, u32[]{:S(2)}) %collective-permute-start.2) | collective-permute-done | bytes 282656 | tf_op jit(solution)/shard_map/ppermute | solution.py:133
  72.8 2.5 collective-permute-start.4
  75.6 1.5 broadcast_in_dim.78
  77.1 11.3 %dynamic_update_slice.24 = bf16[8,141312]{1,0:T(8,128)(2,1)} dynamic-update-slice(bf16[8,141312]{1,0:T(8,128)(2,1)} %broadcast_in_dim.78, bf16[1,141312]{1,0:T(2,128)(2,1)S(1)} %constant_dynamic-update-slice_fusion, s32[]{:T(128)S(6)} %select_n.184, s32[]{:T(128)} %constant.152.clone.1) | dynamic-update-slice | bytes 565252 | tf_op jit(solution)/shard_map/dynamic_update_slice | solution.py:122
  88.6 3.1 %collective-permute-start.5 = (bf16[1,141312]{1,0:T(2,128)(2,1)}, bf16[1,141312]{1,0:T(2,128)(2,1)S(1)}, u32[]{:S(2)}, u32[]{:S(2)}) collective-permute-start(bf16[1,141312]{1,0:T(2,128)(2,1)} %collective-permute-done.3), channel_id=1, source_target_pairs={{0,28},{4,0},{8,4},{12,8},{16,12},{20,16},{24,20},{28,24},{1,29},{... | collective-permute-start | bytes 847880 | tf_op jit(solution)/shard_map/ppermute | solution.py:138
  91.7 11.3 %dynamic_update_slice.25 = bf16[8,141312]{1,0:T(8,128)(2,1)} dynamic-update-slice(bf16[8,141312]{1,0:T(8,128)(2,1)} %dynamic_update_slice.24, bf16[1,141312]{1,0:T(2,128)(2,1)S(1)} %collective-permute-done, s32[]{:T(128)S(6)} %select_n.199, s32[]{:T(128)} %constant.152.clone.1) | dynamic-update-slice | bytes 565252 | tf_op jit(solution)/shard_map/dynamic_update_slice | solution.py:134
  103.0 11.3 %dynamic_update_slice.26 = bf16[8,141312]{1,0:T(8,128)(2,1)} dynamic-update-slice(bf16[8,141312]{1,0:T(8,128)(2,1)} %dynamic_update_slice.25, bf16[1,141312]{1,0:T(2,128)(2,1)S(1)} %collective-permute-done.1, s32[]{:T(128)S(6)} %select_n.201, s32[]{:T(128)} %constant.152.clone.1) | dynamic-update-slice | bytes 565252 | tf_op jit(solution)/shard_map/dynamic_update_slice | solution.py:139
  114.3 11.3 %dynamic_update_slice.27 = bf16[8,141312]{1,0:T(8,128)(2,1)} dynamic-update-slice(bf16[8,141312]{1,0:T(8,128)(2,1)} %dynamic_update_slice.26, bf16[1,141312]{1,0:T(2,128)(2,1)S(1)} %collective-permute-done.2, s32[]{:T(128)S(6)} %select_n.203, s32[]{:T(128)} %constant.152.clone.1) | dynamic-update-slice | bytes 565252 | tf_op jit(solution)/shard_map/dynamic_update_slice | solution.py:134
  125.6 11.3 %dynamic_update_slice.28 = bf16[8,141312]{1,0:T(8,128)(2,1)} dynamic-update-slice(bf16[8,141312]{1,0:T(8,128)(2,1)} %dynamic_update_slice.27, bf16[1,141312]{1,0:T(2,128)(2,1)} %collective-permute-done.3, s32[]{:T(128)S(6)} %select_n.205, s32[]{:T(128)} %constant.152.clone.1) | dynamic-update-slice | bytes 565252 | tf_op jit(solution)/shard_map/dynamic_update_slice | solution.py:139
  136.9 11.3 %dynamic_update_slice.29 = bf16[8,141312]{1,0:T(8,128)(2,1)} dynamic-update-slice(bf16[8,141312]{1,0:T(8,128)(2,1)} %dynamic_update_slice.28, bf16[1,141312]{1,0:T(2,128)(2,1)} %collective-permute-done.4, s32[]{:T(128)S(6)} %select_n.207, s32[]{:T(128)} %constant.152.clone.1) | dynamic-update-slice | bytes 565252 | tf_op jit(solution)/shard_map/dynamic_update_slice | solution.py:134
  148.2 11.3 %dynamic_update_slice.30 = bf16[8,141312]{1,0:T(8,128)(2,1)} dynamic-update-slice(bf16[8,141312]{1,0:T(8,128)(2,1)} %dynamic_update_slice.29, bf16[1,141312]{1,0:T(2,128)(2,1)S(1)} %collective-permute-done.5, s32[]{:T(128)S(6)} %select_n.209, s32[]{:T(128)} %constant.152.clone.1) | dynamic-update-slice | bytes 565252 | tf_op jit(solution)/shard_map/dynamic_update_slice | solution.py:139
  159.5 11.3 %dynamic_update_slice.31 = bf16[8,141312]{1,0:T(8,128)(2,1)} dynamic-update-slice(bf16[8,141312]{1,0:T(8,128)(2,1)} %dynamic_update_slice.30, bf16[1,141312]{1,0:T(2,128)(2,1)S(1)} %collective-permute-done.6, s32[]{:T(128)S(6)} %select_n.211, s32[]{:T(128)} %constant.152.clone.1) | dynamic-update-slice | bytes 565252 | tf_op jit(solution)/shard_map/dynamic_update_slice | solution.py:134
  170.8 1.7 fusion.34
  172.6 1.3 gather_fusion.2
  173.9 2.3 gather_fusion.3
  176.2 1.3 copy.46
  178.1 1.0 bitcast_select_fusion
  179.4 4.5 %maximum_select_fusion = bf16[8,141312]{1,0:T(8,128)(2,1)S(1)} fusion(bf16[8,70656]{1,0:T(8,128)(2,1)} %gather_fusion.3, bf16[8,70656]{1,0:T(8,128)(2,1)S(1)} %gather_fusion.2, pred[8]{0:T(512)(128)(4,1)S(1)} %get-tuple-element.13), kind=kLoop, calls=%fused_computation.15 | loop fusion | flops 5652480 | bytes 4521992 | tf_op jit(solution)/shard_map/jit(_take)/select_n | solution.py:142
  184.0 1.3 copy-done
  185.3 5.0 %reshape.322 = bf16[8,2048,32]{2,1,0:T(8,128)(2,1)} reshape(bf16[8,65536]{1,0:T(8,128)(2,1)S(1)} %slice.44) | data formatting | bytes 2097152 | tf_op jit(solution)/shard_map/reshape | solution.py:29
  190.3 4.6 %copy.49 = bf16[8,2048,32]{1,2,0:T(8,128)(2,1)} copy(bf16[8,2048,32]{2,1,0:T(8,128)(2,1)} %reshape.322) | data formatting | bytes 2097152 | tf_op jit(solution)/shard_map/reshape | solution.py:29
  195.0 1.5 reshape.325
  196.5 0.9 copy.54
  197.4 5.9 %all-gather.2.cloned.1.call-done = bf16[512,2048]{1,0:T(8,128)(2,1)} async-done(((bf16[512,512]{1,0:T(8,128)(2,1)}), bf16[512,2048]{1,0:T(8,128)(2,1)}) %all-gather.2.cloned.1.call-update) | async-done | bytes 2097168 | tf_op jit(solution)/shard_map/all_gather | solution.py:166
  203.3 2.2 fusion
  205.6 2.1 fusion.27
  208.1 1.6 copy-done.10
  209.7 2.4 fusion.29
  212.1 2.4 fusion.25
  216.6 2.3 fusion.35
  218.9 3.5 %fusion.3 = bf16[512,2048]{1,0:T(8,128)(2,1)} fusion(f32[512,2048]{1,0:T(8,128)S(1)} %fusion.35, bf16[1,8,16,2048]{3,1,2,0:T(8,128)(2,1)S(1)} %bitcast.88, f32[512,8,16]{0,2,1:T(8,128)S(1)} %bitcast.101, f32[512,8]{0,1:T(8,128)S(1)} %fusion.19), kind=kOutput, calls=%fused_computation.13 | convolution fusion | flops 1612775424 | bytes 7094272 | tf_op jit(solution)/shard_map/tsr,srd->td/dot_general | solution.py:85
  222.4 31.6 %reduce-scatter.2.cloned.1.call-done = bf16[512,512]{1,0:T(8,128)(2,1)} async-done(((bf16[512,2048]{1,0:T(8,128)(2,1)}), bf16[512,512]{1,0:T(8,128)(2,1)}) %reduce-scatter.2.cloned.1.call-update) | async-done | bytes 524304 | tf_op jit(solution)/shard_map/reduce_scatter | solution.py:170
  254.1 1.8 scatter_fusion
  255.8 1.1 copy.55
  256.9 5.5 %all-to-all-start.1 = ((bf16[2,8,64,512]{3,2,0,1:T(8,128)(2,1)}), bf16[2,8,64,512]{3,2,0,1:T(8,128)(2,1)S(1)}, u32[]{:S(2)}, u32[]{:S(2)}) async-start(bf16[2,8,64,512]{3,2,0,1:T(8,128)(2,1)} %copy.55), calls=%async_computation.2 | async-start | bytes 2097152 | tf_op jit(solution)/shard_map/all_to_all | solution.py:178
  263.7 24.5 %all-to-all-done.1 = bf16[2,8,64,512]{3,2,0,1:T(8,128)(2,1)S(1)} async-done(((bf16[2,8,64,512]{3,2,0,1:T(8,128)(2,1)}), bf16[2,8,64,512]{3,2,0,1:T(8,128)(2,1)S(1)}, u32[]{:S(2)}, u32[]{:S(2)}) %all-to-all-start.1) | async-done | bytes 1048608 | tf_op jit(solution)/shard_map/all_to_all | solution.py:178
  288.7 1.4 fusion.4
  (95 shorter events, 10.4 us)
Async XLA Ops:
  6.5 2.8 copy-start.5
  6.5 3.2 %copy-start.4 = (bf16[1,16,2048]{2,1,0:T(8,128)(2,1)S(1)}, bf16[1,16,2048]{2,1,0:T(8,128)(2,1)}, u32[]{:S(2)}) copy-start(bf16[1,16,2048]{2,1,0:T(8,128)(2,1)} %param.24) | copy-start | bytes 196612
  6.5 9.7 %copy-start.6 = (s32[8,4]{0,1:T(4,128)S(1)}, s32[8,4]{0,1:T(4,128)}, u32[]{:S(2)}) copy-start(s32[8,4]{0,1:T(4,128)} %param.25) | copy-start | bytes 388
  6.5 12.5 %copy-start.1 = (bf16[1024,512]{1,0:T(8,128)(2,1)S(1)}, bf16[1024,512]{1,0:T(8,128)(2,1)}, u32[]{:S(2)}) copy-start(bf16[1024,512]{1,0:T(8,128)(2,1)} %param.16) | copy-start | bytes 3145732
  10.2 35.2 %collective-permute-start = (bf16[1,141312]{1,0:T(2,128)(2,1)S(1)}, bf16[1,141312]{1,0:T(2,128)(2,1)S(1)}, u32[]{:S(2)}, u32[]{:S(2)}) collective-permute-start(bf16[1,141312]{1,0:T(2,128)(2,1)S(1)} %constant_dynamic-update-slice_fusion), channel_id=1, source_target_pairs={{0,4},{4,8},{8,12},{12,16},{16,20},{20,24},{24,28},{28,0},{1,5},{5... | collective-permute-start | bytes 847880 | tf_op jit(solution)/shard_map/ppermute | solution.py:133
  13.2 48.4 %collective-permute-start.1 = (bf16[1,141312]{1,0:T(2,128)(2,1)S(1)}, bf16[1,141312]{1,0:T(2,128)(2,1)S(1)}, u32[]{:S(2)}, u32[]{:S(2)}) collective-permute-start(bf16[1,141312]{1,0:T(2,128)(2,1)S(1)} %constant_dynamic-update-slice_fusion), channel_id=1, source_target_pairs={{0,28},{4,0},{8,4},{12,8},{16,12},{20,16},{24,20},{28,24},{1,29},{... | collective-permute-start | bytes 847880 | tf_op jit(solution)/shard_map/ppermute | solution.py:138
  19.5 5.7 %copy-start.9 = (s32[8]{0:T(128)S(1)}, s32[8]{0:T(128)}, u32[]{:S(2)}) copy-start(s32[8]{0:T(128)} %param.27) | copy-start | bytes 100
  20.5 155.7 %all-to-all-start = ((bf16[2,8,64,512]{3,2,0,1:T(8,128)(2,1)}), bf16[2,8,64,512]{3,2,0,1:T(8,128)(2,1)}, u32[]{:S(2)}, u32[]{:S(2)}) async-start(bf16[2,8,64,512]{3,2,0,1:T(8,128)(2,1)} %copy.45), calls=%async_computation | async-start | bytes 2097152 | tf_op jit(solution)/shard_map/all_to_all | solution.py:153
  24.8 23.4 %copy-start.8 = (s32[8,4]{0,1:T(4,128)S(1)}, s32[8,4]{0,1:T(4,128)}, u32[]{:S(2)}) copy-start(s32[8,4]{0,1:T(4,128)} %param.26) | copy-start | bytes 388
  24.8 178.5 %all-gather.2.cloned.1.call-start = ((), (), s32[]{:S(2)}) async-start(), calls=%async_computation.3 | async-start | bytes 2621440 | tf_op jit(solution)/shard_map/all_gather | solution.py:166
  45.4 27.4 %collective-permute-start.2 = (bf16[1,141312]{1,0:T(2,128)(2,1)S(1)}, bf16[1,141312]{1,0:T(2,128)(2,1)S(1)}, u32[]{:S(2)}, u32[]{:S(2)}) collective-permute-start(bf16[1,141312]{1,0:T(2,128)(2,1)S(1)} %collective-permute-done), channel_id=1, source_target_pairs={{0,4},{4,8},{8,12},{12,16},{16,20},{20,24},{24,28},{28,0},{1,5},{5... | collective-permute-start | bytes 847880 | tf_op jit(solution)/shard_map/ppermute | solution.py:133
  49.6 38.9 %copy-start.7 = (bf16[2048]{0:T(1024)(128)(2,1)S(1)}, bf16[2048]{0:T(1024)(128)(2,1)}, u32[]{:S(2)}) copy-start(bf16[2048]{0:T(1024)(128)(2,1)} %param.17) | copy-start | bytes 12292
  61.5 27.0 %collective-permute-start.3 = (bf16[1,141312]{1,0:T(2,128)(2,1)S(1)}, bf16[1,141312]{1,0:T(2,128)(2,1)}, u32[]{:S(2)}, u32[]{:S(2)}) collective-permute-start(bf16[1,141312]{1,0:T(2,128)(2,1)S(1)} %collective-permute-done.1), channel_id=1, source_target_pairs={{0,28},{4,0},{8,4},{12,8},{16,12},{20,16},{24,20},{28,24},{1,29},{... | collective-permute-start | bytes 847880 | tf_op jit(solution)/shard_map/ppermute | solution.py:138
  72.8 18.9 %collective-permute-start.4 = (bf16[1,141312]{1,0:T(2,128)(2,1)S(1)}, bf16[1,141312]{1,0:T(2,128)(2,1)}, u32[]{:S(2)}, u32[]{:S(2)}) collective-permute-start(bf16[1,141312]{1,0:T(2,128)(2,1)S(1)} %collective-permute-done.2), channel_id=1, source_target_pairs={{0,4},{4,8},{8,12},{12,16},{16,20},{20,24},{24,28},{28,0},{1,5},{5... | collective-permute-start | bytes 847880 | tf_op jit(solution)/shard_map/ppermute | solution.py:133
  88.6 59.7 %collective-permute-start.5 = (bf16[1,141312]{1,0:T(2,128)(2,1)}, bf16[1,141312]{1,0:T(2,128)(2,1)S(1)}, u32[]{:S(2)}, u32[]{:S(2)}) collective-permute-start(bf16[1,141312]{1,0:T(2,128)(2,1)} %collective-permute-done.3), channel_id=1, source_target_pairs={{0,28},{4,0},{8,4},{12,8},{16,12},{20,16},{24,20},{28,24},{1,29},{... | collective-permute-start | bytes 847880 | tf_op jit(solution)/shard_map/ppermute | solution.py:138
  91.7 67.9 %collective-permute-start.6 = (bf16[1,141312]{1,0:T(2,128)(2,1)}, bf16[1,141312]{1,0:T(2,128)(2,1)S(1)}, u32[]{:S(2)}, u32[]{:S(2)}) collective-permute-start(bf16[1,141312]{1,0:T(2,128)(2,1)} %collective-permute-done.4), channel_id=1, source_target_pairs={{0,4},{4,8},{8,12},{12,16},{16,20},{20,24},{24,28},{28,0},{1,5},{5... | collective-permute-start | bytes 847880 | tf_op jit(solution)/shard_map/ppermute | solution.py:133
  179.1 74.8 %reduce-scatter.2.cloned.1.call-start = ((), (), s32[]{:S(2)}) async-start(), calls=%async_computation.4 | async-start | bytes 2621440 | tf_op jit(solution)/shard_map/reduce_scatter | solution.py:170
  183.9 1.4 copy-start
  190.3 4.6 %slice-start = ((bf16[8,141312]{1,0:T(8,128)(2,1)}), bf16[8,28672]{1,0:T(8,128)(2,1)S(1)}, s32[]{:S(2)}) async-start(bf16[8,141312]{1,0:T(8,128)(2,1)} %copy-done), calls=%async_computation.5 | async-start | bytes 917504 | tf_op jit(solution)/shard_map/slice | solution.py:32
  190.3 4.7 %slice-start.1 = ((bf16[8,141312]{1,0:T(8,128)(2,1)}), bf16[8,14336]{1,0:T(8,128)(2,1)S(1)}, s32[]{:S(2)}) async-start(bf16[8,141312]{1,0:T(8,128)(2,1)} %copy-done), calls=%async_computation.6 | async-start | bytes 458752 | tf_op jit(solution)/shard_map/slice | solution.py:35
  203.3 2.2 copy-start.3
  207.7 2.0 copy-start.10
  209.7 2.4 copy-start.11
  214.5 2.0 copy-start.12
  216.6 2.3 slice-start.2
  256.9 31.3 %all-to-all-start.1 = ((bf16[2,8,64,512]{3,2,0,1:T(8,128)(2,1)}), bf16[2,8,64,512]{3,2,0,1:T(8,128)(2,1)S(1)}, u32[]{:S(2)}, u32[]{:S(2)}) async-start(bf16[2,8,64,512]{3,2,0,1:T(8,128)(2,1)} %copy.55), calls=%async_computation.2 | async-start | bytes 2097152 | tf_op jit(solution)/shard_map/all_to_all | solution.py:178
  263.7 25.0 %copy-start.2 = (bf16[1024,512]{1,0:T(8,128)(2,1)S(1)}, bf16[1024,512]{1,0:T(8,128)(2,1)}, u32[]{:S(2)}) copy-start(bf16[1024,512]{1,0:T(8,128)(2,1)} %param.16) | copy-start | bytes 3145732
Sparse Core Ops, SparseCore 0:
  179.3 24.0 all-gather.1
  222.5 31.4 reduce-scatter.1
